TPU v7x, 32 devices: a whole 2x2x4 slice. The times are simulated.
32 devices in a mesh: row: 4 (over y, core), col: 8 (over z, x).
Axes of the slice: x: 2, y: 2, z: 4, core: 2. Of those that a mesh axis runs over, the one named last changes fastest.
Arguments:
- hess_inv: float32 [16384, 16384], P('row', 'col'), as said below
- weights: bfloat16 [6144, 16384], P('row', 'col'), may hold values from -6 to 6
- removed: int32 [128], replicated, may hold values from 0 to 16383, as said below
Outputs:
- hess_out: float32 [16384, 16384], P('row', 'col')
- weight_out: bfloat16 [6144, 16384], P('row', 'col')
Inputs may be any that keep to these rules, and one draw needn't show every extreme that they name: `removed`: sorted ascending and distinct; each aligned block of 2048 columns holds at most 48 of them, and at least one block holds exactly 48. `hess_inv`: symmetric and positive definite.
All inputs are finite; a program needn't handle non-finite values.
Results may differ from a plain program's by a relative error of at most 0.005.
Values may be sent and summed in bfloat16 or wider, within the bound.
No kernel may reach another device: no remote copies, remote signals or barrier semaphores. Data moves between devices by JAX's collectives and lax.ppermute only.
A program may use at most 128 MiB of HBM per device.

v0:
```python
import jax
import jax.numpy as jnp
from jax import lax
from jax.sharding import PartitionSpec as P

MOST = 48


def spread(block, axis, owner):
    block = jnp.where(lax.axis_index(axis) == owner, block, jnp.zeros_like(block))
    return lax.psum(block, axis)


def pick_owned(source, removed, tile_index, tile_size, slot_count, which_axis):
    before = jnp.sum((removed < tile_index * tile_size).astype(jnp.int32))
    within = jnp.sum((removed // tile_size == tile_index).astype(jnp.int32))
    slot_rank = jnp.arange(slot_count, dtype=jnp.int32)
    chosen = jnp.clip(before + slot_rank, 0, removed.shape[0] - 1)
    local_col = jnp.clip(removed[chosen] - tile_index * tile_size, 0, tile_size - 1)
    taken_part = jnp.take(source, local_col, axis=which_axis)
    live_slot = slot_rank < within
    mask_shape = [1, 1]
    mask_shape[which_axis] = slot_count
    return jnp.where(live_slot.reshape(mask_shape), taken_part, jnp.zeros((), taken_part.dtype))


def slot_map(removed, tile_size, slot_count):
    which_tile = removed // tile_size
    first_pos = jnp.sum(
        (removed[None, :] < (which_tile * tile_size)[:, None]).astype(jnp.int32), axis=1
    )
    position = jnp.arange(removed.shape[0], dtype=jnp.int32)
    return which_tile * slot_count + position - first_pos


def on_device(hess_inv, weights, removed):
    row_count = lax.axis_size("row")
    col_count = lax.axis_size("col")
    row_index = lax.axis_index("row")
    col_index = lax.axis_index("col")
    row_tile, col_tile = hess_inv.shape
    tile_ratio = col_count // row_count
    col_slots = slot_map(removed, col_tile, MOST)
    packed_weight = pick_owned(weights, removed, col_index, col_tile, MOST, 1)
    packed_rows = pick_owned(hess_inv, removed, row_index, row_tile, tile_ratio * MOST, 0)
    gathered = lax.all_gather(packed_rows, "row", axis=0, tiled=True)
    upper_rows = jnp.take(gathered, slot_map(removed, row_tile, tile_ratio * MOST), axis=0)
    pieces = [
        spread(upper_rows.astype(jnp.bfloat16), "col", row_index * tile_ratio + offset).astype(
            upper_rows.dtype
        )
        for offset in range(tile_ratio)
    ]
    left_rows = jnp.concatenate(pieces, axis=1)
    weight_wide = lax.all_gather(packed_weight, "col", axis=1, tiled=True)
    weight_left = jnp.take(weight_wide, col_slots, axis=1)
    own_cols = pick_owned(upper_rows, removed, col_index, col_tile, MOST, 1)
    block_wide = lax.all_gather(own_cols, "col", axis=1, tiled=True)
    removed_block = jnp.take(block_wide, col_slots, axis=1)
    factor = jnp.linalg.cholesky(removed_block)
    identity = jnp.eye(removed_block.shape[0], dtype=jnp.float32)
    factor_inv = jax.scipy.linalg.solve_triangular(factor, identity, lower=True)
    block_inv = jnp.dot(factor_inv.T, factor_inv, precision=lax.Precision.HIGHEST)
    coupling = jnp.dot(block_inv, upper_rows, precision=lax.Precision.HIGHEST)
    correction = lax.dot_general(
        left_rows, coupling, (((0,), (0,)), ((), ())), precision=lax.Precision.HIGHEST
    )
    hess_out = hess_inv - correction
    weight_fix = jnp.dot(weight_left.astype(jnp.float32), coupling, precision=lax.Precision.HIGHEST)
    weight_out = (weights.astype(jnp.float32) - weight_fix).astype(jnp.bfloat16)
    return (hess_out, weight_out)


def solution(mesh):
    placed = (P("row", "col"), P("row", "col"), P())
    return jax.shard_map(
        on_device,
        mesh=mesh,
        in_specs=placed,
        out_specs=(P("row", "col"), P("row", "col")),
        check_vma=False,
    )
```

profile of v0, /device:TPU:0, one launch (start us, length us, event | category | flops | bytes accessed | tf_op | source)
XLA Modules:
  0.0 271.6 jit_solution(3088426548601150920)
XLA Ops:
  7.2 0.0 all-gather.5.cloned.1.call-start
  7.2 1.4 fusion.12
  8.6 0.7 fusion.16
  9.3 1.4 gather_fusion.3
  10.8 0.7 iota_compare_fusion.3
  11.4 0.0 copy-start
  11.4 8.6 %copy.13 = bf16[1536,2048]{0,1:T(8,128)(2,1)} copy(bf16[1536,2048]{1,0:T(8,128)(2,1)} %param.4) | data formatting | bytes 12582912 | tf_op args[1]
  20.0 4.4 %gather_fusion.6 = bf16[48,1536]{1,0:T(8,128)(2,1)S(1)} fusion(bf16[1536,2048]{0,1:T(8,128)(2,1)} %copy.13, s32[1024]{0:T(1024)S(1)} %pad_clamp_fusion.1), kind=kCustom, calls=%fused_computation.6 | custom fusion | bytes 295104 | tf_op jit(solution)/shard_map/jit(_take)/gather | solution.py:20
  24.4 0.8 select_bitcast_fusion
  25.2 0.0 all-gather.5.cloned.1.call-update
  25.2 0.0 all-gather.3.cloned.1.call-start
  25.3 0.7 fusion.14
  26.0 0.0 copy-done
  26.0 1.2 gather_fusion
  27.3 11.9 %gather_fusion.1 = f32[96,2048]{1,0:T(8,128)S(1)} fusion(f32[4096,2048]{1,0:T(8,128)} %param.3, s32[1024]{0:T(1024)S(1)} %pad_clamp_fusion.4), kind=kCustom, calls=%fused_computation.1 | custom fusion | bytes 1573248 | tf_op jit(solution)/shard_map/jit(_take)/gather | solution.py:20
  39.2 0.6 fusion.10
  39.8 0.6 iota_compare_fusion.4
  40.5 1.0 select_select_fusion
  41.5 0.0 all-gather.3.cloned.1.call-update
  41.6 0.0 all-reduce.3.cloned.1.call-start
  41.6 0.2 convert_reduce_fusion
  41.9 27.4 %all-gather.5.cloned.1.call-done = bf16[1536,384]{0,1:T(8,128)(2,1)} async-done(((bf16[1536,48]{0,1:T(8,128)(2,1)}), bf16[1536,384]{0,1:T(8,128)(2,1)}) %all-gather.5.cloned.1.call-update) | async-done | bytes 1179664 | tf_op jit(solution)/shard_map/all_gather | solution.py:55
  69.2 2.7 gather_fusion.7
  71.9 26.7 %all-gather.3.cloned.1.call-done = f32[384,2048]{1,0:T(8,128)} async-done(((f32[96,2048]{1,0:T(8,128)}), f32[384,2048]{1,0:T(8,128)}) %all-gather.3.cloned.1.call-update) | async-done | bytes 3145744 | tf_op jit(solution)/shard_map/all_gather | solution.py:46
  98.6 3.3 %gather_fusion.2 = f32[128,2048]{1,0:T(8,128)S(1)} fusion(f32[384,2048]{1,0:T(8,128)} %all-gather.3.cloned.1.call-done, s32[1024]{0:T(1024)S(1)} %pad_clamp_fusion.3), kind=kCustom, calls=%fused_computation.2 | custom fusion | bytes 2097664 | tf_op jit(solution)/shard_map/jit(_take)/gather | solution.py:47
  101.9 1.0 broadcast_select_fusion.2
  102.9 0.3 copy.11
  103.2 0.9 broadcast_select_fusion.1
  104.1 0.6 gather_fusion.4
  104.7 0.1 select_bitcast_fusion.1
  104.8 30.9 %all_gather.10 = f32[128,384]{0,1:T(8,128)S(1)} all-gather(f32[128,48]{0,1:T(8,128)S(1)} %select_bitcast_fusion.1), channel_id=1, replica_groups=mesh['row'=4,'col'=8] {'col'}, dimensions={1}, use_global_device_ids=true | all-gather | bytes 221184 | tf_op jit(solution)/shard_map/all_gather | solution.py:58
  135.7 0.6 gather_fusion.5
  136.3 0.1 broadcast_select_fusion.3
  136.4 0.1 copy.12
  136.5 0.1 fusion.9
  136.6 11.7 %cholesky.16 = f32[128,128]{1,0:T(8,128)S(1)} custom-call(f32[128,128]{1,0:T(8,128)S(1)} %fusion.9), custom_call_target="Cholesky" | custom-call | tf_op jit(solution)/shard_map/jit(cholesky)/cholesky | solution.py:60
  148.3 0.6 compare_reduce_fusion
  149.0 0.7 fusion.6
  149.6 9.8 %custom-call.7 = f32[1,128,128]{1,2,0:T(8,128)S(1)} custom-call(f32[1,128,128]{2,1,0:T(8,128)S(1)} %fusion.6), custom_call_target="InvertDiagBlocksLowerTriangular" | custom-call | tf_op jit(solution)/shard_map/jit(_solve_triangular)/triangular_solve | solution.py:62
  159.5 0.3 fusion.7
  159.7 0.0 all-reduce.3.cloned.1.call-update
  159.7 0.3 fusion.20
  160.0 1.0 fusion.21
  161.0 9.6 %subtract_convert_fusion = bf16[1536,2048]{1,0:T(8,128)(2,1)} fusion(bf16[1536,2048]{1,0:T(8,128)(2,1)} %param.4, f32[128,2048]{1,0:T(8,128)S(1)} %fusion.21, bf16[128,1536]{1,0:T(8,128)(2,1)S(1)} %gather_fusion.7, pred[128]{0:T(512)(128)(4,1)S(1)} %get-tuple-element.10), kind=kOutput, calls=%fused_computation.9 | convolution fusion | flops 4841472000 | bytes 14024832 | tf_op jit(solution)/shard_map/dot_general | solution.py:69
  170.6 67.6 %all-reduce.3.cloned.1.call-done = (bf16[128,2048]{1,0:T(8,128)(2,1)}, bf16[128,2048]{1,0:T(8,128)(2,1)}) async-done(((bf16[128,2048]{1,0:T(8,128)(2,1)}, bf16[128,2048]{1,0:T(8,128)(2,1)}), (bf16[128,2048]{1,0:T(8,128)(2,1)}, bf16[128,2048]{1,0:T(8,128)(2,1)})) %all-reduce.3.cloned.1.call-update) | async-done | bytes 1048592 | tf_op jit(solution)/shard_map/psum | solution.py:11
  238.2 26.9 %convolution_subtract_fusion = f32[4096,2048]{1,0:T(8,128)} fusion(f32[4096,2048]{1,0:T(8,128)} %param.3, f32[128,2048]{1,0:T(8,128)S(1)} %fusion.21, bf16[128,2048]{1,0:T(8,128)(2,1)} %get-tuple-element.6, bf16[128,2048]{1,0:T(8,128)(2,1)} %get-tuple-element.7), kind=kOutput, calls=%fused_computation.8 | convolution fusion | flops 12895387648 | bytes 69206016 | tf_op jit(solution)/shard_map/dot_general | solution.py:65
  (13 shorter events, 0.1 us)
Async XLA Ops:
  7.2 62.1 %all-gather.5.cloned.1.call-start = ((), (), s32[]{:S(2)}) async-start(), calls=%async_computation.1 | async-start | bytes 1327104 | tf_op jit(solution)/shard_map/all_gather | solution.py:55
  11.4 14.6 %copy-start = (s32[128]{0:T(128)S(1)}, s32[128]{0:T(128)}, u32[]{:S(2)}) copy-start(s32[128]{0:T(128)} %param.5) | copy-start | bytes 1540
  25.2 73.4 %all-gather.3.cloned.1.call-start = ((), (), s32[]{:S(2)}) async-start(), calls=%async_computation | async-start | bytes 3932160 | tf_op jit(solution)/shard_map/all_gather | solution.py:46
  41.6 196.6 %all-reduce.3.cloned.1.call-start = ((), (), s32[]{:S(2)}) async-start(), calls=%async_computation.2 | async-start | bytes 2097152 | tf_op jit(solution)/shard_map/psum | solution.py:11
Sparse Core Ops, SparseCore 0:
  25.3 43.8 all-gather.4
  71.4 27.1 all-gather.2
  159.9 78.2 all-reduce.2
where the time goes:
time: 272 us
  waiting for transfers between devices  122 us (45%)
  matrix products  38 us (14%)
  local copies, waits for them, and re-layouts  35.3 us (13%)
  other arithmetic  31.7 us (12%)
  blocking collectives  30.9 us (11%)
  between operations  14 us (5%)
    psum x1, waiting for transfers between devices, spread(): return lax.psum(block, axis)  67.6 us
    all_gather x1, blocking collectives, on_device(): block_wide = lax.all_gather(own_cols, 'col', axis=1, tiled=True)  30.9 us
    all_gather x1, waiting for transfers between devices, on_device(): weight_wide = lax.all_gather(packed_weight, 'col', axis=1, tiled=True)  27.4 us
    dot_general x1, matrix products, on_device(): lax.dot_general(left_rows, coupling, (((0,), (0,)), ((), ())), precision=...  26.9 us
    all_gather x1, waiting for transfers between devices, on_device(): gathered = lax.all_gather(packed_rows, 'row', axis=0, tiled=True)  26.7 us
    gather x3, local copies, waits for them, and re-layouts, pick_owned(): taken_part = jnp.take(source, local_col, axis=which_axis)  16.9 us
    another operation x3, other arithmetic, on_device(): factor = jnp.linalg.cholesky(removed_block)  12.4 us
    another operation x2, other arithmetic, on_device(): factor_inv = jax.scipy.linalg.solve_triangular(factor, identity, lower=True)  10.5 us
  transfers between devices with their start and end apart: 3, of which 3 were waited for; matrix products, arithmetic and copies ran while one was open for 11% of the time, Pallas kernels for 0%

commit v1 on v0

--- a/solution.py
+++ b/solution.py
@@ -4,6 +4,19 @@
 from jax.sharding import PartitionSpec as P
 
 MOST = 48
+
+
+def gather_around(x, axis, dim):
+    ways = lax.axis_size(axis)
+    up = [(d, (d + 1) % ways) for d in range(ways)]
+    down = [(d, (d - 1) % ways) for d in range(ways)]
+    earlier, later = ([x], [x])
+    for _ in range(ways // 2):
+        earlier.append(lax.ppermute(earlier[-1], axis, up))
+    for _ in range((ways - 1) // 2):
+        later.append(lax.ppermute(later[-1], axis, down))
+    line = jnp.concatenate([*earlier[::-1], *later[1:]], axis=dim)
+    return jnp.roll(line, (lax.axis_index(axis) - ways // 2) * x.shape[dim], axis=dim)
 
 
 def spread(block, axis, owner):
@@ -55,7 +68,7 @@
     weight_wide = lax.all_gather(packed_weight, "col", axis=1, tiled=True)
     weight_left = jnp.take(weight_wide, col_slots, axis=1)
     own_cols = pick_owned(upper_rows, removed, col_index, col_tile, MOST, 1)
-    block_wide = lax.all_gather(own_cols, "col", axis=1, tiled=True)
+    block_wide = gather_around(own_cols, "col", 1)
     removed_block = jnp.take(block_wide, col_slots, axis=1)
     factor = jnp.linalg.cholesky(removed_block)
     identity = jnp.eye(removed_block.shape[0], dtype=jnp.float32)

time: 272 us -> 223 us (0.82)
  waiting for transfers between devices: 122 us -> 88.8 us
  blocking collectives: 30.9 us -> 0 us
  starting transfers between devices: 0.12 us -> 13.2 us
    all_gather x1 -> x0, blocking collectives: 30.9 us -> none  [on_device(): block_wide = lax.all_gather(own_cols, 'col', axis=1, tiled=True)]
    psum x1, waiting for transfers between devices: 67.6 us -> 37.8 us  [spread(): return lax.psum(block, axis)]
    ppermute x0 -> x7, starting transfers between devices: none -> 13.1 us  [the longest x3 11.5 us: gather_around(): later.append(lax.ppermute(later[-1], axis, down))]
    all_gather x1, waiting for transfers between devices: 26.7 us -> 16 us  [on_device(): gathered = lax.all_gather(packed_rows, 'row', axis=0, tiled=True)]
    ppermute x0 -> x7, waiting for transfers between devices: none -> 9.18 us  [the longest x4 6.91 us: gather_around(): earlier.append(lax.ppermute(earlier[-1], axis, up))]
    unnamed x3 -> x16, local copies, waits for them, and re-layouts: 8.62 us -> 8.67 us
  transfers between devices with their start and end apart: 3 -> 10, of which waited for: 3 -> 7; matrix products, arithmetic and copies ran while one was open for 11% -> 27% of each run, Pallas kernels for 0% -> 0%
where the time goes in v1:
time: 223 us; the launch traced here: 222 us
  waiting for transfers between devices  88.8 us (40%)
  matrix products  38 us (17%)
  local copies, waits for them, and re-layouts  36.2 us (16%)
  other arithmetic  31.7 us (14%)
  between operations  14.1 us (6%)
  starting transfers between devices  13.2 us (6%)
    psum x1, waiting for transfers between devices, spread(): return lax.psum(block, axis)  37.8 us
    dot_general x1, matrix products, on_device(): lax.dot_general(left_rows, coupling, (((0,), (0,)), ((), ())), precision=...  26.9 us
    all_gather x1, waiting for transfers between devices, on_device(): weight_wide = lax.all_gather(packed_weight, 'col', axis=1, tiled=True)  25.8 us
    gather x3, local copies, waits for them, and re-layouts, pick_owned(): taken_part = jnp.take(source, local_col, axis=which_axis)  17.4 us
    all_gather x1, waiting for transfers between devices, on_device(): gathered = lax.all_gather(packed_rows, 'row', axis=0, tiled=True)  16 us
    another operation x3, other arithmetic, on_device(): factor = jnp.linalg.cholesky(removed_block)  12.4 us
    ppermute x3, starting transfers between devices, gather_around(): later.append(lax.ppermute(later[-1], axis, down))  11.5 us
    another operation x2, other arithmetic, on_device(): factor_inv = jax.scipy.linalg.solve_triangular(factor, identity, lower=True)  10.5 us
  transfers between devices with their start and end apart: 10, of which 7 were waited for; matrix products, arithmetic and copies ran while one was open for 27% of the time, Pallas kernels for 0%

profile of v1, /device:TPU:0, one launch (start us, length us, event | category | flops | bytes accessed | tf_op | source)
XLA Modules:
  0.0 222.0 jit_solution(3103524658662190716)
XLA Ops:
  7.2 1.3 fusion.12
  8.6 0.7 fusion.14
  9.2 1.6 gather_fusion
  10.8 0.7 fusion.16
  11.5 1.4 gather_fusion.3
  13.0 0.6 fusion.10
  13.6 0.6 iota_compare_fusion.4
  14.3 11.8 %gather_fusion.1 = f32[96,2048]{1,0:T(8,128)S(1)} fusion(f32[4096,2048]{1,0:T(8,128)} %param.3, s32[1024]{0:T(1024)S(1)} %get-tuple-element.25), kind=kCustom, calls=%fused_computation.1 | custom fusion | bytes 1573248 | tf_op jit(solution)/shard_map/jit(_take)/gather | solution.py:33
  26.0 1.0 select_select_fusion
  27.2 8.6 %copy.13 = bf16[1536,2048]{0,1:T(8,128)(2,1)} copy(bf16[1536,2048]{1,0:T(8,128)(2,1)} %param.4) | data formatting | bytes 12582912 | tf_op args[1]
  35.8 5.1 %gather_fusion.6 = bf16[48,1536]{1,0:T(8,128)(2,1)S(1)} fusion(bf16[1536,2048]{0,1:T(8,128)(2,1)} %copy.13, s32[1024]{0:T(1024)S(1)} %get-tuple-element.24), kind=kCustom, calls=%fused_computation.6 | custom fusion | bytes 295104 | tf_op jit(solution)/shard_map/jit(_take)/gather | solution.py:33
  40.9 0.5 iota_compare_fusion.3
  41.4 0.8 select_bitcast_fusion
  42.2 0.0 all-reduce.3.cloned.1.call-start
  42.3 0.2 convert_reduce_fusion
  42.5 16.0 %all-gather.3.cloned.1.call-done = f32[384,2048]{1,0:T(8,128)} async-done(((f32[96,2048]{1,0:T(8,128)}), f32[384,2048]{1,0:T(8,128)}) %all-gather.3.cloned.1.call-update) | async-done | bytes 3145744 | tf_op jit(solution)/shard_map/all_gather | solution.py:59
  58.5 3.3 %gather_fusion.2 = f32[128,2048]{1,0:T(8,128)S(1)} fusion(f32[384,2048]{1,0:T(8,128)} %all-gather.3.cloned.1.call-done, s32[1024]{0:T(1024)S(1)} %pad_clamp_fusion.3), kind=kCustom, calls=%fused_computation.2 | custom fusion | bytes 2097664 | tf_op jit(solution)/shard_map/jit(_take)/gather | solution.py:60
  61.8 1.0 broadcast_select_fusion.2
  62.8 0.3 copy.11
  63.2 0.6 gather_fusion.4
  63.7 0.1 select_bitcast_fusion.1
  63.8 1.5 collective-permute-start
  65.3 5.1 %collective-permute-done = f32[128,48]{0,1:T(8,128)S(1)} collective-permute-done((f32[128,48]{0,1:T(8,128)S(1)}, f32[128,48]{0,1:T(8,128)S(1)}, u32[]{:S(2)}, u32[]{:S(2)}) %collective-permute-start) | collective-permute-done | bytes 24608 | tf_op jit(solution)/shard_map/ppermute | solution.py:15
  70.4 4.8 %collective-permute-start.4 = (f32[128,48]{0,1:T(8,128)S(1)}, f32[128,48]{0,1:T(8,128)S(1)}, u32[]{:S(2)}, u32[]{:S(2)}) collective-permute-start(f32[128,48]{0,1:T(8,128)S(1)} %select_bitcast_fusion.1), channel_id=1, source_target_pairs={{0,7},{1,0},{2,1},{3,2},{4,3},{5,4},{6,5},{7,6},{8,15},{9,8},{10,9... | collective-permute-start | bytes 73736 | tf_op jit(solution)/shard_map/ppermute | solution.py:17
  75.2 1.8 collective-permute-done.1
  77.1 25.8 %all-gather.5.cloned.1.call-done = bf16[1536,384]{0,1:T(8,128)(2,1)} async-done(((bf16[1536,48]{0,1:T(8,128)(2,1)}), bf16[1536,384]{0,1:T(8,128)(2,1)}) %all-gather.5.cloned.1.call-update) | async-done | bytes 1179664 | tf_op jit(solution)/shard_map/all_gather | solution.py:68
  102.9 2.7 %gather_fusion.7 = bf16[128,1536]{1,0:T(8,128)(2,1)S(1)} fusion(bf16[1536,384]{0,1:T(8,128)(2,1)} %all-gather.5.cloned.1.call-done, s32[1024]{0:T(1024)S(1)} %pad_clamp_fusion), kind=kCustom, calls=%fused_computation.7 | custom fusion | bytes 786944 | tf_op jit(solution)/shard_map/jit(_take)/gather | solution.py:69
  105.6 2.1 collective-permute-start.5
  107.7 0.9 broadcast_select_fusion.1
  108.6 0.9 collective-permute-done.5
  109.5 4.7 %collective-permute-start.6 = (f32[128,48]{0,1:T(8,128)S(1)}, f32[128,48]{0,1:T(8,128)S(1)}, u32[]{:S(2)}, u32[]{:S(2)}) collective-permute-start(f32[128,48]{0,1:T(8,128)S(1)} %collective-permute-done.5), channel_id=1, source_target_pairs={{0,7},{1,0},{2,1},{3,2},{4,3},{5,4},{6,5},{7,6},{8,15},{9,8},{10,9... | collective-permute-start | bytes 73736 | tf_op jit(solution)/shard_map/ppermute | solution.py:17
  114.2 0.1 constant_dynamic-update-slice_fusion.11
  114.3 1.4 collective-permute-done.6
  115.7 0.1 constant_dynamic-update-slice_fusion.3
  115.9 0.6 gather_fusion.5
  116.5 0.1 broadcast_select_fusion.3
  116.6 0.1 copy.12
  116.7 0.1 fusion.9
  116.8 11.7 %cholesky.16 = f32[128,128]{1,0:T(8,128)S(1)} custom-call(f32[128,128]{1,0:T(8,128)S(1)} %fusion.9), custom_call_target="Cholesky" | custom-call | tf_op jit(solution)/shard_map/jit(cholesky)/cholesky | solution.py:73
  128.6 0.6 compare_reduce_fusion
  129.2 0.7 fusion.6
  129.9 9.8 %custom-call.7 = f32[1,128,128]{1,2,0:T(8,128)S(1)} custom-call(f32[1,128,128]{2,1,0:T(8,128)S(1)} %fusion.6), custom_call_target="InvertDiagBlocksLowerTriangular" | custom-call | tf_op jit(solution)/shard_map/jit(_solve_triangular)/triangular_solve | solution.py:75
  139.7 0.2 fusion.7
  139.9 0.3 fusion.20
  140.2 1.0 fusion.21
  141.3 9.6 %subtract_convert_fusion = bf16[1536,2048]{1,0:T(8,128)(2,1)} fusion(bf16[1536,2048]{1,0:T(8,128)(2,1)} %param.4, f32[128,2048]{1,0:T(8,128)S(1)} %fusion.21, bf16[128,1536]{1,0:T(8,128)(2,1)S(1)} %gather_fusion.7, pred[128]{0:T(512)(128)(4,1)S(1)} %get-tuple-element.10), kind=kOutput, calls=%fused_computation.9 | convolution fusion | flops 4841472000 | bytes 14024832 | tf_op jit(solution)/shard_map/dot_general | solution.py:82
  150.8 37.8 %all-reduce.3.cloned.1.call-done = (bf16[128,2048]{1,0:T(8,128)(2,1)}, bf16[128,2048]{1,0:T(8,128)(2,1)}) async-done(((bf16[128,2048]{1,0:T(8,128)(2,1)}, bf16[128,2048]{1,0:T(8,128)(2,1)}), (bf16[128,2048]{1,0:T(8,128)(2,1)}, bf16[128,2048]{1,0:T(8,128)(2,1)})) %all-reduce.3.cloned.1.call-update) | async-done | bytes 1048592 | tf_op jit(solution)/shard_map/psum | solution.py:24
  188.6 26.9 %convolution_subtract_fusion = f32[4096,2048]{1,0:T(8,128)} fusion(f32[4096,2048]{1,0:T(8,128)} %param.3, f32[128,2048]{1,0:T(8,128)S(1)} %fusion.21, bf16[128,2048]{1,0:T(8,128)(2,1)} %get-tuple-element.6, bf16[128,2048]{1,0:T(8,128)(2,1)} %get-tuple-element.7), kind=kOutput, calls=%fused_computation.8 | convolution fusion | flops 12895387648 | bytes 69206016 | tf_op jit(solution)/shard_map/dot_general | solution.py:78
  (40 shorter events, 0.4 us)
Async XLA Ops:
  7.2 51.3 %all-gather.3.cloned.1.call-start = ((), (), s32[]{:S(2)}) async-start(), calls=%async_computation | async-start | bytes 3932160 | tf_op jit(solution)/shard_map/all_gather | solution.py:59
  27.1 15.2 %copy-start = (s32[128]{0:T(128)S(1)}, s32[128]{0:T(128)}, u32[]{:S(2)}) copy-start(s32[128]{0:T(128)} %param.5) | copy-start | bytes 1540
  27.1 75.8 %all-gather.5.cloned.1.call-start = ((), (), s32[]{:S(2)}) async-start(), calls=%async_computation.1 | async-start | bytes 1327104 | tf_op jit(solution)/shard_map/all_gather | solution.py:68
  42.2 146.4 %all-reduce.3.cloned.1.call-start = ((), (), s32[]{:S(2)}) async-start(), calls=%async_computation.2 | async-start | bytes 2097152 | tf_op jit(solution)/shard_map/psum | solution.py:24
  63.8 6.6 %collective-permute-start = (f32[128,48]{0,1:T(8,128)S(1)}, f32[128,48]{0,1:T(8,128)S(1)}, u32[]{:S(2)}, u32[]{:S(2)}) collective-permute-start(f32[128,48]{0,1:T(8,128)S(1)} %select_bitcast_fusion.1), channel_id=1, source_target_pairs={{0,1},{1,2},{2,3},{3,4},{4,5},{5,6},{6,7},{7,0},{8,9},{9,10},{10,1... | collective-permute-start | bytes 73736 | tf_op jit(solution)/shard_map/ppermute | solution.py:15
  70.4 6.6 %collective-permute-start.1 = (f32[128,48]{0,1:T(8,128)S(1)}, f32[128,48]{0,1:T(8,128)S(1)}, u32[]{:S(2)}, u32[]{:S(2)}) collective-permute-start(f32[128,48]{0,1:T(8,128)S(1)} %collective-permute-done), channel_id=1, source_target_pairs={{0,1},{1,2},{2,3},{3,4},{4,5},{5,6},{6,7},{7,0},{8,9},{9,10},{10,1... | collective-permute-start | bytes 73736 | tf_op jit(solution)/shard_map/ppermute | solution.py:15
  70.4 35.2 %collective-permute-start.4 = (f32[128,48]{0,1:T(8,128)S(1)}, f32[128,48]{0,1:T(8,128)S(1)}, u32[]{:S(2)}, u32[]{:S(2)}) collective-permute-start(f32[128,48]{0,1:T(8,128)S(1)} %select_bitcast_fusion.1), channel_id=1, source_target_pairs={{0,7},{1,0},{2,1},{3,2},{4,3},{5,4},{6,5},{7,6},{8,15},{9,8},{10,9... | collective-permute-start | bytes 73736 | tf_op jit(solution)/shard_map/ppermute | solution.py:17
  77.0 30.6 %collective-permute-start.2 = (f32[128,48]{0,1:T(8,128)S(1)}, f32[128,48]{0,1:T(8,128)S(1)}, u32[]{:S(2)}, u32[]{:S(2)}) collective-permute-start(f32[128,48]{0,1:T(8,128)S(1)} %collective-permute-done.1), channel_id=1, source_target_pairs={{0,1},{1,2},{2,3},{3,4},{4,5},{5,6},{6,7},{7,0},{8,9},{9,10},{10,1... | collective-permute-start | bytes 73736 | tf_op jit(solution)/shard_map/ppermute | solution.py:15
  105.6 3.9 %collective-permute-start.5 = (f32[128,48]{0,1:T(8,128)S(1)}, f32[128,48]{0,1:T(8,128)S(1)}, u32[]{:S(2)}, u32[]{:S(2)}) collective-permute-start(f32[128,48]{0,1:T(8,128)S(1)} %collective-permute-done.4), channel_id=1, source_target_pairs={{0,7},{1,0},{2,1},{3,2},{4,3},{5,4},{6,5},{7,6},{8,15},{9,8},{10,9... | collective-permute-start | bytes 73736 | tf_op jit(solution)/shard_map/ppermute | solution.py:17
  107.7 6.5 %collective-permute-start.3 = (f32[128,48]{0,1:T(8,128)S(1)}, f32[128,48]{0,1:T(8,128)S(1)}, u32[]{:S(2)}, u32[]{:S(2)}) collective-permute-start(f32[128,48]{0,1:T(8,128)S(1)} %collective-permute-done.2), channel_id=1, source_target_pairs={{0,1},{1,2},{2,3},{3,4},{4,5},{5,6},{6,7},{7,0},{8,9},{9,10},{10,1... | collective-permute-start | bytes 73736 | tf_op jit(solution)/shard_map/ppermute | solution.py:15
  109.5 6.2 %collective-permute-start.6 = (f32[128,48]{0,1:T(8,128)S(1)}, f32[128,48]{0,1:T(8,128)S(1)}, u32[]{:S(2)}, u32[]{:S(2)}) collective-permute-start(f32[128,48]{0,1:T(8,128)S(1)} %collective-permute-done.5), channel_id=1, source_target_pairs={{0,7},{1,0},{2,1},{3,2},{4,3},{5,4},{6,5},{7,6},{8,15},{9,8},{10,9... | collective-permute-start | bytes 73736 | tf_op jit(solution)/shard_map/ppermute | solution.py:17
Sparse Core Ops, SparseCore 0:
  27.2 31.2 all-gather.2
  61.3 41.5 all-gather.4
  108.7 79.8 all-reduce.2
